TPU v7x, 32 devices: a whole 2x2x4 slice. The times are simulated.
32 devices in a mesh: grp: 2 (over y), blk: 8 (over z, x), seq: 1, ch: 2 (over core).
Axes of the slice: x: 2, y: 2, z: 4, core: 2. Of those that a mesh axis runs over, the one named last changes fastest.
Arguments:
- alignment_activity: bfloat16 [512, 128, 64], P(('grp', 'seq'), 'blk'), parts along dimension 0, may hold values from -40 to 40
- sequence_mask: int32 [512], P('grp'), parts along dimension 0, may hold values 0 or 1
- residue_mask: int32 [256], P('grp'), parts along dimension 0, may hold values 0 or 1
- lower_weights: bfloat16 [64, 32], replicated, may hold values from -0.75 to 0.75
- upper_weights: bfloat16 [64, 32], replicated, may hold values from -0.75 to 0.75
- output_projector: bfloat16 [1024, 128], replicated, may hold values from -0.1875 to 0.1875
Outputs:
- pair_update: bfloat16 [128, 256, 128], P('ch', ('grp', 'blk'), 'seq'), parts along dimension 1
There are 2 independent parts, one for each index of `grp`. A program takes and returns all parts, laid end to end along the dimension named above; an argument that names none is the same for every part. Nothing has to cross between parts.
All inputs are finite; a program needn't handle non-finite values.
Results may differ from a plain program's by a relative error of at most 0.012.
Values may be sent and summed in bfloat16 or wider, within the bound.
A program may use at most 64 MiB of HBM per device.

v0:
```python
import math

import jax
import jax.numpy as jnp
from jax import lax
from jax.sharding import PartitionSpec as P


def shards(
    alignment_activity, sequence_mask, residue_mask, lower_weights, upper_weights, output_projector
):
    local_rows, block_rows, channel_count = alignment_activity.shape
    proj_width = lower_weights.shape[1]
    pair_width = output_projector.shape[1]
    seq_count = lax.axis_size("seq")
    core_count = lax.axis_size("ch")
    seq_place = lax.axis_index("seq")
    blk_place = lax.axis_index("blk")
    core_place = lax.axis_index("ch")
    value_entries = alignment_activity.astype(jnp.float32)
    centred = value_entries - jnp.mean(value_entries, axis=-1, keepdims=True)
    variance = jnp.mean(centred * centred, axis=-1, keepdims=True)
    normed = (centred * lax.rsqrt(variance + 1e-05)).astype(jnp.bfloat16)
    rows_valid = lax.dynamic_slice_in_dim(sequence_mask, seq_place * local_rows, local_rows).astype(
        jnp.float32
    )
    res_valid = lax.dynamic_slice_in_dim(residue_mask, blk_place * block_rows, block_rows).astype(
        jnp.float32
    )
    weight = (rows_valid[:, None] * res_valid[None, :])[:, :, None]
    left_matrix = (
        jnp.einsum("sic,cd->sid", normed, lower_weights, preferred_element_type=jnp.float32)
        * weight
    ).astype(jnp.bfloat16)
    right = (
        jnp.einsum("sic,cd->sid", normed, upper_weights, preferred_element_type=jnp.float32)
        * weight
    ).astype(jnp.bfloat16)
    right_flat = right.reshape(local_rows, block_rows * proj_width)
    table = output_projector.reshape(proj_width, proj_width, pair_width)
    out_width = pair_width // core_count
    table_used = lax.dynamic_slice_in_dim(table, core_place * out_width, out_width, 2)
    used_channels = table_used.shape[2]
    piece = lax.all_gather(right_flat, "blk", axis=1, tiled=True)
    col_count = piece.shape[1] // proj_width
    block_cols = math.gcd(col_count, 128)
    block_count = col_count // block_cols
    stacked = piece.reshape(local_rows, block_count, block_cols, proj_width).transpose(1, 0, 2, 3)

    def one_block(right_part):
        outer = jnp.einsum(
            "sic,sjd->ijcd", left_matrix, right_part, preferred_element_type=jnp.float32
        ).astype(jnp.bfloat16)
        return jnp.einsum("ijcd,cde->eij", outer, table_used, preferred_element_type=jnp.float32)

    results = lax.map(one_block, stacked)
    partial_sum = results.transpose(1, 2, 0, 3).reshape(used_channels, block_rows, col_count)
    all_cols = partial_sum.shape[2]
    quarter_cols = all_cols // seq_count
    summed = lax.psum_scatter(
        partial_sum.astype(jnp.bfloat16), "seq", scatter_dimension=2, tiled=True
    ).astype(jnp.float32)
    count = jnp.sum(sequence_mask.astype(jnp.float32))
    col_valid = lax.dynamic_slice_in_dim(
        residue_mask, seq_place * quarter_cols, quarter_cols
    ).astype(jnp.float32)
    norm = res_valid[:, None] * col_valid[None, :] * count
    return (summed / jnp.maximum(norm, 1.0)[None]).astype(jnp.bfloat16)


def solution(mesh):
    in_specs = (P(("grp", "seq"), "blk", None), P("grp"), P("grp"), P(), P(), P())
    out_specs = P("ch", ("grp", "blk"), "seq")
    return jax.shard_map(shards, mesh=mesh, in_specs=in_specs, out_specs=out_specs, check_vma=False)
```

profile of v0, /device:TPU:0, one launch (start us, length us, event | category | flops | bytes accessed | tf_op | source)
XLA Modules:
  0.0 110.0 jit_solution(18392558506096459744)
XLA Ops:
  6.5 0.0 copy-start
  6.5 0.0 all-gather.2.cloned.1.call-start
  6.5 1.2 %convert_reduce_fusion = f32[256,16]{0,1:T(8,128)S(1)} fusion(bf16[256,16,64]{0,2,1:T(8,128)(2,1)} %param.6), kind=kLoop, calls=%fused_computation.4 | loop fusion | flops 520192 | bytes 540672 | tf_op jit(solution)/shard_map/reduce_sum | solution.py:21
  7.7 1.2 %fusion.23 = f32[256,16]{0,1:T(8,128)S(1)} fusion(bf16[256,16,64]{0,2,1:T(8,128)(2,1)} %param.6, f32[256,16]{0,1:T(8,128)S(1)} %broadcast_multiply_fusion.1), kind=kLoop, calls=%fused_computation.17 | loop fusion | flops 1044480 | bytes 557056 | tf_op jit(solution)/shard_map/reduce_sum | solution.py:22
  8.9 0.7 convert_element_type.40
  9.6 0.7 dynamic-slice_convert_fusion
  10.4 0.1 add_rsqrt_fusion
  10.4 2.0 %fusion.20 = bf16[256,16,32]{0,2,1:T(8,128)(2,1)} fusion(bf16[256,16,64]{0,2,1:T(8,128)(2,1)} %param.6, f32[256,16]{0,1:T(8,128)S(1)} %get-tuple-element.13, f32[256,16]{0,1:T(8,128)S(1)} %broadcast_multiply_fusion.1, f32[256,16]{0,1:T(8,128)S(1)} %get-tuple-element.14, bf16[64,32]{0,1:T(8,128)(2,1)} %param.10), kind=kOutput, calls=%fused_computation.14 | convolution fusion | flops 18087936 | bytes 839680 | tf_op jit(solution)/shard_map/sic,cd->sid/dot_general | solution.py:36
  12.5 0.0 all-gather.2.cloned.1.call-update
  12.5 0.7 convert_element_type.48
  13.1 1.4 %convert_reduce_fusion.1 = f32[]{:T(128)} fusion(s32[256]{0:T(256)} %param.7), kind=kLoop, calls=%fused_computation.31 | loop fusion | flops 511 | bytes 1028 | tf_op jit(solution)/shard_map/reduce_sum | solution.py:63
  14.5 0.8 multiply_maximum_fusion
  15.3 49.4 %all-gather.2.cloned.1.call-done = bf16[256,4096]{0,1:T(8,128)(2,1)} async-done(((bf16[256,512]{0,1:T(8,128)(2,1)}), bf16[256,4096]{0,1:T(8,128)(2,1)}) %all-gather.2.cloned.1.call-update) | async-done | bytes 2097168 | tf_op jit(solution)/shard_map/all_gather | solution.py:44
  64.6 9.9 %fusion.25 = bf16[128,32,16,32]{3,1,2,0:T(8,128)(2,1)} fusion(bf16[256,128,32,1]{0,2,3,1:T(8,128)(2,1)} %bitcast.47, bf16[256,16,64]{0,2,1:T(8,128)(2,1)} %param.6, f32[256,16]{0,1:T(8,128)S(1)} %get-tuple-element.13, f32[256,16]{0,1:T(8,128)S(1)} %broadcast_multiply_fusion.1, f32[256,16]{0,1:T(8,128)S(1)} %get-tuple-element.14, bf16[64,32]{0,1:T(8,128)(2,1)} %param.9), kind=kOutput, calls=%fused_computation.19 | convolution fusion | flops 1091829760 | bytes 6868992 | tf_op jit(solution)/shard_map/while/body/eval_jaxpr/sic,sjd->ijcd/dot_general | solution.py:51
  74.6 24.6 %copy.9 = bf16[128,32,16,32]{0,1,3,2:T(8,128)(2,1)} copy(bf16[128,32,16,32]{3,1,2,0:T(8,128)(2,1)} %fusion.25) | data formatting | bytes 8388608 | tf_op jit(solution)/shard_map/while/body/eval_jaxpr/sic,sjd->ijcd/dot_general | solution.py:51
  99.2 0.0 copy-done
  99.2 3.1 %fusion.17 = bf16[64,16,128]{2,0,1:T(8,128)(2,1)S(1)} fusion(bf16[128,32,16,32]{0,1,3,2:T(8,128)(2,1)} %copy.9, f32[16,128]{1,0:T(8,128)S(1)} %multiply_maximum_fusion, bf16[32,32,128]{2,1,0:T(8,128)(2,1)S(1)} %bitcast.46, s32[]{:T(128)S(6)} %select_n.8), kind=kOutput, calls=%fused_computation.13 | convolution fusion | flops 268959744 | bytes 4726788 | tf_op jit(solution)/shard_map/while/body/eval_jaxpr/ijcd,cde->eij/dot_general | solution.py:54
  102.3 0.9 copy.7
  (1 shorter events, 0.0 us)
Async XLA Ops:
  6.5 92.6 %copy-start = (bf16[1024,128]{1,0:T(8,128)(2,1)S(1)}, bf16[1024,128]{1,0:T(8,128)(2,1)}, u32[]{:S(2)}) copy-start(bf16[1024,128]{1,0:T(8,128)(2,1)} %param.11) | copy-start | bytes 786436
  6.5 58.1 %all-gather.2.cloned.1.call-start = ((), (), s32[]{:S(2)}) async-start(), calls=%async_computation | async-start | bytes 2359296 | tf_op jit(solution)/shard_map/all_gather | solution.py:44
Sparse Core Ops, SparseCore 0:
  12.6 51.9 all-gather.1
where the time goes:
time: 110 us
  waiting for transfers between devices  49.4 us (45%)
  local copies, waits for them, and re-layouts  25.5 us (23%)
  matrix products  15.1 us (14%)
  between operations  13.4 us (12%)
  other arithmetic  6.66 us (6%)
    all_gather x1, waiting for transfers between devices, shards(): piece = lax.all_gather(right_flat, 'blk', axis=1, tiled=True)  49.4 us
    dot_general x1, local copies, waits for them, and re-layouts, one_block(): jnp.einsum('sic,sjd->ijcd', left_matrix, right_part, preferred_element_ty...  24.6 us
    dot_general x1, matrix products, one_block(): jnp.einsum('sic,sjd->ijcd', left_matrix, right_part, preferred_element_ty...  9.94 us
    dot_general x1, matrix products, one_block(): jnp.einsum('ijcd,cde->eij', outer, table_used, preferred_element_type=jnp...  3.13 us
  transfers between devices with their start and end apart: 1, of which 1 were waited for; matrix products, arithmetic and copies ran while one was open for 3% of the time, Pallas kernels for 0%

commit v1 on v0

--- a/solution.py
+++ b/solution.py
@@ -1,8 +1,11 @@
+import functools
 import math
 
 import jax
 import jax.numpy as jnp
 from jax import lax
+from jax.experimental import pallas as pl
+from jax.experimental.pallas import tpu as pltpu
 from jax.sharding import PartitionSpec as P
 
 
@@ -68,7 +71,270 @@
     return (summed / jnp.maximum(norm, 1.0)[None]).astype(jnp.bfloat16)
 
 
+F32 = jnp.float32
+BF16 = jnp.bfloat16
+CHUNKS = 2
+MESH = pl.DeviceIdType.MESH
+
+
+def fused(
+    sizes,
+    x_ref, srow_ref, jrow_ref, rmask_ref, lower_ref, upper_ref, table_ref,
+    out_ref,
+    wide, left_t, right_w, right_t, table_w, acc, away, near, inv,
+    recv_sem, send_sem, swap_sem,
+):
+    nblk, rows, res, feat, width = sizes
+    half = width // 2
+    part = half // CHUNKS
+    nz = nblk // 2
+    cols = nblk * res
+    lane_tiles = rows // 128
+    blk = lax.axis_index("blk")
+    core = lax.axis_index("ch")
+    z = blk // 2
+    side = blk % 2
+    across = z * 2 + 1 - side
+
+    barrier = pltpu.get_barrier_semaphore()
+    pl.semaphore_signal(barrier, inc=1, device_id={"blk": across}, device_id_type=MESH)
+    pl.semaphore_signal(barrier, inc=1, device_id={"ch": 1 - core}, device_id_type=MESH)
+
+    @pl.when(z > 0)
+    def _():
+        pl.semaphore_signal(barrier, inc=1, device_id={"blk": blk - 2}, device_id_type=MESH)
+
+    @pl.when(z < nz - 1)
+    def _():
+        pl.semaphore_signal(barrier, inc=1, device_id={"blk": blk + 2}, device_id_type=MESH)
+
+    wide[:, :feat] = x_ref[...].astype(F32).reshape(rows * res, feat)
+    r_at = lax.broadcasted_iota(jnp.int32, (feat, feat), 0)
+    c_at = lax.broadcasted_iota(jnp.int32, (feat, feat), 1)
+    centre = (jnp.where(r_at == c_at, 1.0, 0.0) - 1.0 / feat).astype(BF16)
+    lower_t = lower_ref[...].astype(F32).T.astype(BF16)
+    upper_t = upper_ref[...].astype(F32).T.astype(BF16)
+    weights = jnp.concatenate([lower_t, upper_t], axis=0)
+    srow = srow_ref[...].astype(F32)
+    nt = (((1,), (1,)), ((), ()))
+    for i in range(res):
+        x_i = wide[pl.ds(i, rows, stride=res), :][:, :feat].astype(BF16)
+        cent = lax.dot_general(centre, x_i, nt, preferred_element_type=F32)
+        var = jnp.mean(cent * cent, axis=0, keepdims=True)
+        normed = (cent * lax.rsqrt(var + 1e-05)).astype(BF16)
+        proj = jnp.dot(weights, normed, preferred_element_type=F32)
+        proj = proj * (srow * rmask_ref[blk * res + i].astype(F32))
+        left_t[i * width:(i + 1) * width, :] = proj[:width].astype(BF16)
+        for g in range(lane_tiles):
+            right_w[g, pl.ds(i, width, stride=res), :] = proj[width:, g * 128:(g + 1) * 128]
+    mine = pl.ds(pl.multiple_of(core * (half * res), half * res), half * res)
+    for g in range(lane_tiles):
+        block = right_w[g, mine, :].astype(BF16).reshape(half, res, 128)
+        right_t[blk, :, :, g * 128:(g + 1) * 128] = block
+
+    peers = 2 + (z + nz - 1) // nz + (2 * nz - 2 - z) // nz
+    pl.semaphore_wait(barrier, peers)
+
+    def copy(block, q, way, target):
+        ref = right_t.at[block, pl.ds(q * part, part)]
+        return pltpu.make_async_remote_copy(
+            src_ref=ref, dst_ref=ref,
+            send_sem=send_sem.at[way, block, q], recv_sem=recv_sem.at[block, q],
+            device_id={"blk": target}, device_id_type=MESH,
+        )
+
+    def up(block, q):
+        return copy(block, q, 0, blk + 2)
+
+    def down(block, q):
+        return copy(block, q, 1, blk - 2)
+
+    def cross(block, q):
+        return copy(block, q, 2, across)
+
+    def each_hop(q, hop, act_below, act_above):
+        @pl.when(z >= hop)
+        def _():
+            act_below(blk - 2 * hop, q)
+
+        @pl.when(z + hop < nz)
+        def _():
+            act_above(blk + 2 * hop, q)
+
+    for q in range(CHUNKS):
+        cross(blk, q).start()
+
+        @pl.when(z < nz - 1)
+        def _():
+            up(blk, q).start()
+
+        @pl.when(z > 0)
+        def _():
+            down(blk, q).start()
+
+    table_w[...] = table_ref[...].astype(F32)
+    pieces = [table_w[pl.ds(core * half + k, width, stride=width), :] for k in range(half)]
+    table_t = jnp.concatenate(pieces, axis=0).T.astype(BF16)
+    jrow = jrow_ref[...].astype(F32)
+    count = jnp.sum(srow, axis=1, keepdims=True)
+    for i in range(res):
+        norm = jrow * rmask_ref[blk * res + i].astype(F32) * count
+        inv[i:i + 1, :] = 1.0 / jnp.maximum(norm, 1.0)
+
+    def from_below(block, q):
+        copy(block, q, 0, blk).wait_recv()
+        cross(block, q).start()
+
+        @pl.when(z < nz - 1)
+        def _():
+            up(block, q).start()
+
+    def from_above(block, q):
+        copy(block, q, 1, blk).wait_recv()
+        cross(block, q).start()
+
+        @pl.when(z > 0)
+        def _():
+            down(block, q).start()
+
+    for hop in range(1, nz):
+        for q in range(CHUNKS):
+            each_hop(q, hop, from_below, from_above)
+
+    pairs = res // 2
+    for q in range(CHUNKS):
+        for k in range(nz):
+            copy(2 * k + 1 - side, q, 2, blk).wait_recv()
+        base = q * part
+        right_q = jnp.concatenate(
+            [right_t[:, base + k].reshape(cols, rows) for k in range(part)], axis=0
+        )
+        table_q = table_t[:, base * width:(base + part) * width]
+        for p in range(pairs):
+            left_p = left_t[p * 2 * width:(p + 1) * 2 * width, :]
+            outer = lax.dot_general(left_p, right_q, nt, preferred_element_type=F32).astype(BF16)
+            both = [
+                jnp.concatenate(
+                    [
+                        outer[u * width:(u + 1) * width, k * cols:(k + 1) * cols]
+                        for k in range(part)
+                    ],
+                    axis=0,
+                )
+                for u in range(2)
+            ]
+            term = jnp.dot(table_q, jnp.concatenate(both, axis=1), preferred_element_type=F32)
+            for u in range(2):
+                at = pl.ds(p * 2 + u, table_t.shape[0], stride=res)
+                piece = term[:, u * cols:(u + 1) * cols]
+                if q == 0:
+                    acc[at, :] = piece
+                else:
+                    acc[at, :] += piece
+
+    count_rows = acc.shape[0] // 2
+    other = pl.multiple_of((1 - core) * count_rows, count_rows)
+    own = pl.multiple_of(core * count_rows, count_rows)
+    away[...] = acc[pl.ds(other, count_rows), :].astype(away.dtype)
+    swap = pltpu.make_async_remote_copy(
+        src_ref=away, dst_ref=near, send_sem=swap_sem.at[0], recv_sem=swap_sem.at[1],
+        device_id={"ch": 1 - core}, device_id_type=MESH,
+    )
+    swap.start()
+
+    def sent_below(block, q):
+        cross(block, q).wait_send()
+
+        @pl.when(z < nz - 1)
+        def _():
+            up(block, q).wait_send()
+
+    def sent_above(block, q):
+        cross(block, q).wait_send()
+
+        @pl.when(z > 0)
+        def _():
+            down(block, q).wait_send()
+
+    for q in range(CHUNKS):
+        cross(blk, q).wait_send()
+
+        @pl.when(z < nz - 1)
+        def _():
+            up(blk, q).wait_send()
+
+        @pl.when(z > 0)
+        def _():
+            down(blk, q).wait_send()
+
+        for hop in range(1, nz):
+            each_hop(q, hop, sent_below, sent_above)
+
+    swap.wait()
+    total = acc[pl.ds(own, count_rows), :] + near[...].astype(F32)
+    total = total.reshape(count_rows // res, res, cols) * inv[...][None]
+    out_ref[...] = total.astype(BF16)
+
+
+def fused_shards(
+    alignment_activity, sequence_mask, residue_mask, lower_weights, upper_weights, output_projector
+):
+    rows, res, feat = alignment_activity.shape
+    width = lower_weights.shape[1]
+    pair = output_projector.shape[1]
+    nblk = lax.axis_size("blk")
+    cols = nblk * res
+    half = width // 2
+    vmem = pl.BlockSpec(memory_space=pltpu.VMEM)
+    return pl.pallas_call(
+        functools.partial(fused, (nblk, rows, res, feat, width)),
+        out_shape=jax.ShapeDtypeStruct((pair // 2, res, cols), BF16),
+        in_specs=[vmem, vmem, vmem, pl.BlockSpec(memory_space=pltpu.SMEM), vmem, vmem, vmem],
+        out_specs=vmem,
+        scratch_shapes=[
+            pltpu.VMEM((rows * res, 128), F32),
+            pltpu.VMEM((res * width, rows), BF16),
+            pltpu.VMEM((rows // 128, width * res, 128), F32),
+            pltpu.VMEM((nblk, half, res, rows), BF16),
+            pltpu.VMEM((width * width, pair), F32),
+            pltpu.VMEM((pair * res, cols), F32),
+            pltpu.VMEM((pair // 2 * res, cols), SWAP_TYPE),
+            pltpu.VMEM((pair // 2 * res, cols), SWAP_TYPE),
+            pltpu.VMEM((res, cols), F32),
+            pltpu.SemaphoreType.DMA((nblk, CHUNKS)),
+            pltpu.SemaphoreType.DMA((3, nblk, CHUNKS)),
+            pltpu.SemaphoreType.DMA((2,)),
+        ],
+        compiler_params=pltpu.CompilerParams(
+            collective_id=0, has_side_effects=True, vmem_limit_bytes=40 * 1024 * 1024
+        ),
+        name="outer_product_mean",
+    )(
+        alignment_activity,
+        sequence_mask.reshape(1, rows),
+        residue_mask.reshape(1, cols),
+        residue_mask,
+        lower_weights,
+        upper_weights,
+        output_projector,
+    )
+
+
+SWAP_TYPE = F32
+
+
+def choose(*arrays):
+    rows, res, _ = arrays[0].shape
+    width = arrays[3].shape[1]
+    nblk = lax.axis_size("blk")
+    one_share = lax.axis_size("seq") == 1 and lax.axis_size("ch") == 2
+    tiled = nblk % 2 == 0 and nblk * res == 128 and res % 16 == 0 and rows % 128 == 0
+    if one_share and tiled and width % 32 == 0:
+        return fused_shards(*arrays)
+    return shards(*arrays)
+
+
 def solution(mesh):
     in_specs = (P(("grp", "seq"), "blk", None), P("grp"), P("grp"), P(), P(), P())
     out_specs = P("ch", ("grp", "blk"), "seq")
-    return jax.shard_map(shards, mesh=mesh, in_specs=in_specs, out_specs=out_specs, check_vma=False)
+    return jax.shard_map(choose, mesh=mesh, in_specs=in_specs, out_specs=out_specs, check_vma=False)

time: 110 us -> 32.6 us (0.30)
  waiting for transfers between devices: 49.4 us -> 0 us
  Pallas kernels: 0 us -> 28.6 us
  local copies, waits for them, and re-layouts: 25.5 us -> 3.66 us
  matrix products: 15.1 us -> 0 us
  between operations: 13.4 us -> 0.07 us
  other arithmetic: 6.66 us -> 0 us
    all_gather x1 -> x0, waiting for transfers between devices: 49.4 us -> none  [shards(): piece = lax.all_gather(right_flat, 'blk', axis=1, tiled=True)]
    pallas_call x0 -> x1, Pallas kernels: none -> 28.6 us  [fused_shards(): pl.pallas_call(functools.partial(fused, (nblk, rows, res, feat, width)),...]
    dot_general x1 -> x0, local copies, waits for them, and re-layouts: 24.6 us -> none  [one_block(): jnp.einsum('sic,sjd->ijcd', left_matrix, right_part, preferred_element_ty...]
    dot_general x3 -> x0, matrix products: 15.1 us -> none  [the longest x1 9.94 us: one_block(): jnp.einsum('sic,sjd->ijcd', left_matrix, right_part, preferred_element_ty...]
    reduce_sum x3 -> x0, other arithmetic: 3.75 us -> none  [the longest x1 1.36 us: shards(): count = jnp.sum(sequence_mask.astype(jnp.float32))]
    unnamed x2 -> x12, local copies, waits for them, and re-layouts: 0.01 us -> 3.66 us
    convert_element_type x3 -> x0, other arithmetic: 2.07 us -> none  [the longest x1 0.73 us: shards(): lax.dynamic_slice_in_dim(residue_mask, blk_place * block_rows, block_rows)]
  transfers between devices with their start and end apart: 1 -> 0, of which waited for: 1 -> 0; matrix products, arithmetic and copies ran while one was open for 3% -> 0% of each run, Pallas kernels for 0% -> 0%
where the time goes in v1:
time: 32.6 us; the launch traced here: 32.4 us
  Pallas kernels  28.6 us (88%)
  local copies, waits for them, and re-layouts  3.66 us (11%)
    pallas_call x1, Pallas kernels, fused_shards(): pl.pallas_call(functools.partial(fused, (nblk, rows, res, feat, width)),...  28.6 us
    unnamed x12, local copies, waits for them, and re-layouts  3.66 us

profile of v1, /device:TPU:0, one launch (start us, length us, event | category | flops | bytes accessed | tf_op | source)
XLA Modules:
  0.0 32.4 jit_solution(1478229420345598130)
XLA Ops:
  0.0 0.0 copy-start.3
  0.0 0.8 %copy.8.lower_ref = bf16[64,32]{1,0:T(8,128)(2,1)S(1)} copy(bf16[64,32]{0,1:T(8,128)(2,1)} %param.9) | data formatting | bytes 8192 | tf_op args[3]
  0.8 0.0 copy-done.3
  0.8 0.1 copy.9.upper_ref
  0.9 0.0 copy-start
  0.9 0.0 copy-start.1
  0.9 0.0 copy-start.2
  0.9 2.0 %copy.7.x_ref = bf16[256,16,64]{2,1,0:T(8,128)(2,1)S(1)} copy(bf16[256,16,64]{0,2,1:T(8,128)(2,1)} %param.6) | data formatting | bytes 1048576 | tf_op args[0]
  3.0 0.0 copy-done
  3.0 0.0 copy-done.1
  3.0 0.0 copy-done.2
  3.0 28.6 %outer_product_mean.1 = bf16[64,16,128]{2,1,0:T(8,128)(2,1)S(1)} custom-call(bf16[256,16,64]{2,1,0:T(8,128)(2,1)S(1)} %copy.7.x_ref, s32[1,256]{1,0:T(1,128)S(1)} %bitcast.3, s32[1,128]{1,0:T(1,128)S(1)} %bitcast.2, s32[128]{0:T(128)S(1)} %copy-done.1, bf16[64,32]{1,0:T(8,128)(2,1)S(1)} %copy.8.lower_ref, bf16[64,32]{1,0:T(8,128)(2,1)S(1)} %copy.9.upper_ref, ...), custom_call_target="tpu_custom_call" | custom-call | tf_op jit(solution)/shard_map/outer_product_mean/pallas_call | solution.py:289
  31.7 0.7 %copy.11 = bf16[64,16,128]{2,1,0:T(8,128)(2,1)} copy(bf16[64,16,128]{2,1,0:T(8,128)(2,1)S(1)} %outer_product_mean.1) | data formatting | bytes 524288
Async XLA Ops:
  0.0 0.8 %copy-start.3 = (bf16[64,32]{0,1:T(8,128)(2,1)S(1)}, bf16[64,32]{0,1:T(8,128)(2,1)}, u32[]{:S(2)}) copy-start(bf16[64,32]{0,1:T(8,128)(2,1)} %param.10) | copy-start | bytes 12292
  0.9 2.1 %copy-start = (bf16[1024,128]{1,0:T(8,128)(2,1)S(1)}, bf16[1024,128]{1,0:T(8,128)(2,1)}, u32[]{:S(2)}) copy-start(bf16[1024,128]{1,0:T(8,128)(2,1)} %table_ref.1) | copy-start | bytes 786436
  0.9 2.1 %copy-start.1 = (s32[128]{0:T(128)S(1)}, s32[128]{0:T(128)}, u32[]{:S(2)}) copy-start(s32[128]{0:T(128)} %rmask_ref.1) | copy-start | bytes 1540
  0.9 2.1 %copy-start.2 = (s32[256]{0:T(256)S(1)}, s32[256]{0:T(256)}, u32[]{:S(2)}) copy-start(s32[256]{0:T(256)} %param.7) | copy-start | bytes 3076

commit v2 on v1

--- a/solution.py
+++ b/solution.py
@@ -74,15 +74,17 @@
 F32 = jnp.float32
 BF16 = jnp.bfloat16
 CHUNKS = 2
+VMEM_BYTES = 63 * 1024 * 1024
 MESH = pl.DeviceIdType.MESH
 
 
 def fused(
     sizes,
-    x_ref, srow_ref, jrow_ref, rmask_ref, lower_ref, upper_ref, table_ref,
+    x_hbm, srow_hbm, jrow_hbm, rmask_hbm, lower_hbm, upper_hbm, table_hbm,
     out_ref,
-    wide, left_t, right_w, right_t, table_w, acc, away, near, inv,
-    recv_sem, send_sem, swap_sem,
+    x_ref, srow_ref, jrow_ref, rmask_ref, lower_ref, upper_ref, table_ref, normed_ref, left_t, right_w, right_t, table_w, outer_ref,
+    acc, away, near, inv,
+    load_sem, recv_sem, send_sem, swap_sem,
 ):
     nblk, rows, res, feat, width = sizes
     half = width // 2
@@ -90,6 +92,8 @@
     nz = nblk // 2
     cols = nblk * res
     lane_tiles = rows // 128
+    groups = 4
+    group = res // groups
     blk = lax.axis_index("blk")
     core = lax.axis_index("ch")
     z = blk // 2
@@ -108,25 +112,35 @@
     def _():
         pl.semaphore_signal(barrier, inc=1, device_id={"blk": blk + 2}, device_id_type=MESH)
 
-    wide[:, :feat] = x_ref[...].astype(F32).reshape(rows * res, feat)
-    r_at = lax.broadcasted_iota(jnp.int32, (feat, feat), 0)
-    c_at = lax.broadcasted_iota(jnp.int32, (feat, feat), 1)
-    centre = (jnp.where(r_at == c_at, 1.0, 0.0) - 1.0 / feat).astype(BF16)
-    lower_t = lower_ref[...].astype(F32).T.astype(BF16)
-    upper_t = upper_ref[...].astype(F32).T.astype(BF16)
-    weights = jnp.concatenate([lower_t, upper_t], axis=0)
+    loads = [
+        pltpu.make_async_copy(x_hbm.at[pl.ds(g * group, group)], x_ref.at[pl.ds(g * group, group)], load_sem.at[g])
+        for g in range(groups)
+    ]
+    early = ((upper_hbm, upper_ref), (srow_hbm, srow_ref), (rmask_hbm, rmask_ref))
+    later = ((lower_hbm, lower_ref), (jrow_hbm, jrow_ref), (table_hbm, table_ref))
+    smalls = [
+        pltpu.make_async_copy(src, dst, load_sem.at[groups + k])
+        for k, (src, dst) in enumerate(early + later)
+    ]
+    for load in smalls[:3] + loads + smalls[3:]:
+        load.start()
+    for load in smalls[:3]:
+        load.wait()
+
     srow = srow_ref[...].astype(F32)
-    nt = (((1,), (1,)), ((), ()))
+    upper_t = upper_ref[...]
     for i in range(res):
-        x_i = wide[pl.ds(i, rows, stride=res), :][:, :feat].astype(BF16)
-        cent = lax.dot_general(centre, x_i, nt, preferred_element_type=F32)
+        if i % group == 0:
+            loads[i // group].wait()
+        x_i = x_ref[i].astype(F32)
+        cent = x_i - jnp.mean(x_i, axis=0, keepdims=True)
         var = jnp.mean(cent * cent, axis=0, keepdims=True)
         normed = (cent * lax.rsqrt(var + 1e-05)).astype(BF16)
-        proj = jnp.dot(weights, normed, preferred_element_type=F32)
+        normed_ref[i] = normed
+        proj = jnp.dot(upper_t, normed, preferred_element_type=F32)
         proj = proj * (srow * rmask_ref[blk * res + i].astype(F32))
-        left_t[i * width:(i + 1) * width, :] = proj[:width].astype(BF16)
         for g in range(lane_tiles):
-            right_w[g, pl.ds(i, width, stride=res), :] = proj[width:, g * 128:(g + 1) * 128]
+            right_w[g, pl.ds(i, width, stride=res), :] = proj[:, g * 128:(g + 1) * 128]
     mine = pl.ds(pl.multiple_of(core * (half * res), half * res), half * res)
     for g in range(lane_tiles):
         block = right_w[g, mine, :].astype(BF16).reshape(half, res, 128)
@@ -171,6 +185,14 @@
         @pl.when(z > 0)
         def _():
             down(blk, q).start()
+
+    for load in smalls[3:]:
+        load.wait()
+    lower_t = lower_ref[...]
+    for i in range(res):
+        proj = jnp.dot(lower_t, normed_ref[i], preferred_element_type=F32)
+        proj = proj * (srow * rmask_ref[blk * res + i].astype(F32))
+        left_t[i * width:(i + 1) * width, :] = proj.astype(BF16)
 
     table_w[...] = table_ref[...].astype(F32)
     pieces = [table_w[pl.ds(core * half + k, width, stride=width), :] for k in range(half)]
@@ -201,27 +223,25 @@
         for q in range(CHUNKS):
             each_hop(q, hop, from_below, from_above)
 
+    nt = (((1,), (1,)), ((), ()))
     pairs = res // 2
     for q in range(CHUNKS):
         for k in range(nz):
             copy(2 * k + 1 - side, q, 2, blk).wait_recv()
         base = q * part
-        right_q = jnp.concatenate(
-            [right_t[:, base + k].reshape(cols, rows) for k in range(part)], axis=0
-        )
+        for k in range(base, base + part, 2):
+            right_k = jnp.concatenate(
+                [right_t[:, k + u].reshape(cols, rows) for u in range(2)], axis=0
+            )
+            outer = lax.dot_general(left_t[...], right_k, nt, preferred_element_type=F32)
+            outer = outer.astype(BF16)
+            for u in range(2):
+                piece = outer[:, u * cols:(u + 1) * cols].reshape(res, width, cols)
+                outer_ref[:, (k + u) * width:(k + u + 1) * width, :] = piece
         table_q = table_t[:, base * width:(base + part) * width]
         for p in range(pairs):
-            left_p = left_t[p * 2 * width:(p + 1) * 2 * width, :]
-            outer = lax.dot_general(left_p, right_q, nt, preferred_element_type=F32).astype(BF16)
             both = [
-                jnp.concatenate(
-                    [
-                        outer[u * width:(u + 1) * width, k * cols:(k + 1) * cols]
-                        for k in range(part)
-                    ],
-                    axis=0,
-                )
-                for u in range(2)
+                outer_ref[p * 2 + u, base * width:(base + part) * width, :] for u in range(2)
             ]
             term = jnp.dot(table_q, jnp.concatenate(both, axis=1), preferred_element_type=F32)
             for u in range(2):
@@ -286,36 +306,46 @@
     cols = nblk * res
     half = width // 2
     vmem = pl.BlockSpec(memory_space=pltpu.VMEM)
+    hbm = pl.BlockSpec(memory_space=pltpu.HBM)
     return pl.pallas_call(
         functools.partial(fused, (nblk, rows, res, feat, width)),
         out_shape=jax.ShapeDtypeStruct((pair // 2, res, cols), BF16),
-        in_specs=[vmem, vmem, vmem, pl.BlockSpec(memory_space=pltpu.SMEM), vmem, vmem, vmem],
+        in_specs=[hbm] * 7,
         out_specs=vmem,
         scratch_shapes=[
-            pltpu.VMEM((rows * res, 128), F32),
+            pltpu.VMEM((res, feat, rows), BF16),
+            pltpu.VMEM((1, rows), jnp.int32),
+            pltpu.VMEM((1, cols), jnp.int32),
+            pltpu.SMEM((cols,), jnp.int32),
+            pltpu.VMEM((width, feat), BF16),
+            pltpu.VMEM((width, feat), BF16),
+            pltpu.VMEM((width * width, pair), BF16),
+            pltpu.VMEM((res, feat, rows), BF16),
             pltpu.VMEM((res * width, rows), BF16),
             pltpu.VMEM((rows // 128, width * res, 128), F32),
             pltpu.VMEM((nblk, half, res, rows), BF16),
             pltpu.VMEM((width * width, pair), F32),
+            pltpu.VMEM((res, half * width, cols), BF16),
             pltpu.VMEM((pair * res, cols), F32),
             pltpu.VMEM((pair // 2 * res, cols), SWAP_TYPE),
             pltpu.VMEM((pair // 2 * res, cols), SWAP_TYPE),
             pltpu.VMEM((res, cols), F32),
+            pltpu.SemaphoreType.DMA((10,)),
             pltpu.SemaphoreType.DMA((nblk, CHUNKS)),
             pltpu.SemaphoreType.DMA((3, nblk, CHUNKS)),
             pltpu.SemaphoreType.DMA((2,)),
         ],
         compiler_params=pltpu.CompilerParams(
-            collective_id=0, has_side_effects=True, vmem_limit_bytes=40 * 1024 * 1024
+            collective_id=0, has_side_effects=True, vmem_limit_bytes=VMEM_BYTES
         ),
         name="outer_product_mean",
     )(
-        alignment_activity,
+        alignment_activity.transpose(1, 2, 0),
         sequence_mask.reshape(1, rows),
         residue_mask.reshape(1, cols),
         residue_mask,
-        lower_weights,
-        upper_weights,
+        lower_weights.T,
+        upper_weights.T,
         output_projector,
     )
 

time: 32.6 us -> 25.9 us (0.79)
  Pallas kernels: 28.6 us -> 24.1 us
  local copies, waits for them, and re-layouts: 3.66 us -> 1.67 us
    pallas_call x1, Pallas kernels: 28.6 us -> 24.1 us  [fused_shards(): pl.pallas_call(functools.partial(fused, (nblk, rows, res, feat, width)),...]
    unnamed x12 -> x1, local copies, waits for them, and re-layouts: 3.66 us -> 1.67 us
where the time goes in v2:
time: 25.9 us; the launch traced here: 25.7 us
  Pallas kernels  24.1 us (93%)
  local copies, waits for them, and re-layouts  1.67 us (6%)
    pallas_call x1, Pallas kernels, fused_shards(): pl.pallas_call(functools.partial(fused, (nblk, rows, res, feat, width)),...  24.1 us
    unnamed x1, local copies, waits for them, and re-layouts  1.67 us

profile of v2, /device:TPU:0, one launch (start us, length us, event | category | flops | bytes accessed | tf_op | source)
XLA Modules:
  0.0 25.7 jit_solution(487760527425214057)
XLA Ops:
  0.0 24.1 %outer_product_mean.1 = bf16[64,16,128]{2,1,0:T(8,128)(2,1)} custom-call(bf16[16,64,256]{2,1,0:T(8,128)(2,1)} %bitcast.5, s32[1,256]{1,0:T(1,128)} %bitcast.9, s32[1,128]{1,0:T(1,128)} %bitcast.8, s32[128]{0:T(128)} %rmask_hbm.1, bf16[32,64]{1,0:T(8,128)(2,1)} %bitcast.6, bf16[32,64]{1,0:T(8,128)(2,1)} %bitcast.7, bf16[1024,128]{1,0:T(8,128)(2,1)} %table_hbm.1), custom_call_target="tpu_custom_call" | custom-call | tf_op jit(solution)/shard_map/outer_product_mean/pallas_call | solution.py:310
  24.1 1.7 %copy.8 = bf16[64,16,128]{2,1,0:T(8,128)(2,1)} copy(bf16[64,16,128]{2,1,0:T(8,128)(2,1)} %outer_product_mean.1) | data formatting | bytes 524288

commit v3 on v2

--- a/solution.py
+++ b/solution.py
@@ -83,7 +83,7 @@
     x_hbm, srow_hbm, jrow_hbm, rmask_hbm, lower_hbm, upper_hbm, table_hbm,
     out_ref,
     x_ref, srow_ref, jrow_ref, rmask_ref, lower_ref, upper_ref, table_ref, normed_ref, left_t, right_w, right_t, table_w, outer_ref,
-    acc, away, near, inv,
+    acc, near, inv,
     load_sem, recv_sem, send_sem, swap_sem,
 ):
     nblk, rows, res, feat, width = sizes
@@ -169,11 +169,11 @@
     def each_hop(q, hop, act_below, act_above):
         @pl.when(z >= hop)
         def _():
-            act_below(blk - 2 * hop, q)
+            act_below(blk - 2 * hop, q, hop)
 
         @pl.when(z + hop < nz)
         def _():
-            act_above(blk + 2 * hop, q)
+            act_above(blk + 2 * hop, q, hop)
 
     for q in range(CHUNKS):
         cross(blk, q).start()
@@ -196,24 +196,51 @@
 
     table_w[...] = table_ref[...].astype(F32)
     pieces = [table_w[pl.ds(core * half + k, width, stride=width), :] for k in range(half)]
-    table_t = jnp.concatenate(pieces, axis=0).T.astype(BF16)
+    pair = table_w.shape[1]
+    turned = pltpu.roll(jnp.concatenate(pieces, axis=0), core * (pair // 2), axis=1)
+    table_t = turned.T.astype(BF16)
     jrow = jrow_ref[...].astype(F32)
     count = jnp.sum(srow, axis=1, keepdims=True)
     for i in range(res):
         norm = jrow * rmask_ref[blk * res + i].astype(F32) * count
         inv[i:i + 1, :] = 1.0 / jnp.maximum(norm, 1.0)
 
-    def from_below(block, q):
+    even = z % 2 == 0
+    last = CHUNKS - 1
+    mate = blk + 2 - 4 * (z % 2)
+
+    def relay(block):
+        return copy(block, last, 3, mate)
+
+    def cross_below(block, q, hop, act):
+        if hop == 1 and q == last:
+            pl.when(even)(lambda: act(cross(block, q)))
+        else:
+            act(cross(block, q))
+
+    def cross_above(block, q, hop, act):
+        if hop == 1 and q == last:
+            pl.when(z % 2 == 1)(lambda: act(cross(block, q)))
+        else:
+            act(cross(block, q))
+
+    def start(made):
+        made.start()
+
+    def sent(made):
+        made.wait_send()
+
+    def from_below(block, q, hop):
         copy(block, q, 0, blk).wait_recv()
-        cross(block, q).start()
+        cross_below(block, q, hop, start)
 
         @pl.when(z < nz - 1)
         def _():
             up(block, q).start()
 
-    def from_above(block, q):
+    def from_above(block, q, hop):
         copy(block, q, 1, blk).wait_recv()
-        cross(block, q).start()
+        cross_above(block, q, hop, start)
 
         @pl.when(z > 0)
         def _():
@@ -222,12 +249,27 @@
     for hop in range(1, nz):
         for q in range(CHUNKS):
             each_hop(q, hop, from_below, from_above)
+        if hop == 1:
+            copy(across, last, 2, blk).wait_recv()
+            relay(across).start()
+
+    def swap(h):
+        return pltpu.make_async_remote_copy(
+            src_ref=acc.at[1, h], dst_ref=near.at[h],
+            send_sem=swap_sem.at[0, h], recv_sem=swap_sem.at[1, h],
+            device_id={"ch": 1 - core}, device_id_type=MESH,
+        )
 
     nt = (((1,), (1,)), ((), ()))
     pairs = res // 2
     for q in range(CHUNKS):
         for k in range(nz):
-            copy(2 * k + 1 - side, q, 2, blk).wait_recv()
+            if q == last:
+                @pl.when(z != k)
+                def _():
+                    copy(2 * k + 1 - side, q, 2, blk).wait_recv()
+            else:
+                copy(2 * k + 1 - side, q, 2, blk).wait_recv()
         base = q * part
         for k in range(base, base + part, 2):
             right_k = jnp.concatenate(
@@ -245,32 +287,25 @@
             ]
             term = jnp.dot(table_q, jnp.concatenate(both, axis=1), preferred_element_type=F32)
             for u in range(2):
-                at = pl.ds(p * 2 + u, table_t.shape[0], stride=res)
-                piece = term[:, u * cols:(u + 1) * cols]
-                if q == 0:
-                    acc[at, :] = piece
-                else:
-                    acc[at, :] += piece
-
-    count_rows = acc.shape[0] // 2
-    other = pl.multiple_of((1 - core) * count_rows, count_rows)
-    own = pl.multiple_of(core * count_rows, count_rows)
-    away[...] = acc[pl.ds(other, count_rows), :].astype(away.dtype)
-    swap = pltpu.make_async_remote_copy(
-        src_ref=away, dst_ref=near, send_sem=swap_sem.at[0], recv_sem=swap_sem.at[1],
-        device_id={"ch": 1 - core}, device_id_type=MESH,
-    )
-    swap.start()
-
-    def sent_below(block, q):
-        cross(block, q).wait_send()
+                i = p * 2 + u
+                at = pl.ds(i % 8, pair // 2, stride=8)
+                for g in range(2):
+                    piece = term[g * (pair // 2):(g + 1) * (pair // 2), u * cols:(u + 1) * cols]
+                    if q > 0:
+                        piece = piece + acc[g, i // 8, at, :]
+                    acc[g, i // 8, at, :] = piece
+            if q == last and p % 4 == 3:
+                swap(p // 4).start()
+
+    def sent_below(block, q, hop):
+        cross_below(block, q, hop, sent)
 
         @pl.when(z < nz - 1)
         def _():
             up(block, q).wait_send()
 
-    def sent_above(block, q):
-        cross(block, q).wait_send()
+    def sent_above(block, q, hop):
+        cross_above(block, q, hop, sent)
 
         @pl.when(z > 0)
         def _():
@@ -289,11 +324,14 @@
 
         for hop in range(1, nz):
             each_hop(q, hop, sent_below, sent_above)
-
-    swap.wait()
-    total = acc[pl.ds(own, count_rows), :] + near[...].astype(F32)
-    total = total.reshape(count_rows // res, res, cols) * inv[...][None]
-    out_ref[...] = total.astype(BF16)
+    relay(across).wait_send()
+
+    sums = []
+    for h in range(res // 8):
+        swap(h).wait()
+        total = (acc[0, h] + near[h]).reshape(pair // 2, 8, cols)
+        sums.append(total * inv[h * 8:(h + 1) * 8, :][None])
+    out_ref[...] = jnp.concatenate(sums, axis=1).astype(BF16)
 
 
 def fused_shards(
@@ -326,14 +364,13 @@
             pltpu.VMEM((nblk, half, res, rows), BF16),
             pltpu.VMEM((width * width, pair), F32),
             pltpu.VMEM((res, half * width, cols), BF16),
-            pltpu.VMEM((pair * res, cols), F32),
-            pltpu.VMEM((pair // 2 * res, cols), SWAP_TYPE),
-            pltpu.VMEM((pair // 2 * res, cols), SWAP_TYPE),
+            pltpu.VMEM((2, res // 8, pair // 2 * 8, cols), F32),
+            pltpu.VMEM((res // 8, pair // 2 * 8, cols), F32),
             pltpu.VMEM((res, cols), F32),
             pltpu.SemaphoreType.DMA((10,)),
             pltpu.SemaphoreType.DMA((nblk, CHUNKS)),
-            pltpu.SemaphoreType.DMA((3, nblk, CHUNKS)),
-            pltpu.SemaphoreType.DMA((2,)),
+            pltpu.SemaphoreType.DMA((4, nblk, CHUNKS)),
+            pltpu.SemaphoreType.DMA((2, res // 8)),
         ],
         compiler_params=pltpu.CompilerParams(
             collective_id=0, has_side_effects=True, vmem_limit_bytes=VMEM_BYTES
@@ -350,15 +387,12 @@
     )
 
 
-SWAP_TYPE = F32
-
-
 def choose(*arrays):
     rows, res, _ = arrays[0].shape
     width = arrays[3].shape[1]
     nblk = lax.axis_size("blk")
     one_share = lax.axis_size("seq") == 1 and lax.axis_size("ch") == 2
-    tiled = nblk % 2 == 0 and nblk * res == 128 and res % 16 == 0 and rows % 128 == 0
+    tiled = nblk % 4 == 0 and nblk * res == 128 and res % 16 == 0 and rows % 128 == 0
     if one_share and tiled and width % 32 == 0:
         return fused_shards(*arrays)
     return shards(*arrays)

time: 25.9 us -> 25.8 us (level)
  no operation moved by 1% of the time
where the time goes in v3:
time: 25.8 us; the launch traced here: 25.6 us
  Pallas kernels  24 us (93%)
  local copies, waits for them, and re-layouts  1.67 us (6%)
    pallas_call x1, Pallas kernels, fused_shards(): pl.pallas_call(functools.partial(fused, (nblk, rows, res, feat, width)),...  24 us
    unnamed x1, local copies, waits for them, and re-layouts  1.67 us

profile of v3, /device:TPU:0, one launch (start us, length us, event | category | flops | bytes accessed | tf_op | source)
XLA Modules:
  0.0 25.6 jit_solution(1335932431822048658)
XLA Ops:
  0.0 24.0 %outer_product_mean.1 = bf16[64,16,128]{2,1,0:T(8,128)(2,1)} custom-call(bf16[16,64,256]{2,1,0:T(8,128)(2,1)} %bitcast.5, s32[1,256]{1,0:T(1,128)} %bitcast.9, s32[1,128]{1,0:T(1,128)} %bitcast.8, s32[128]{0:T(128)} %rmask_hbm.1, bf16[32,64]{1,0:T(8,128)(2,1)} %bitcast.6, bf16[32,64]{1,0:T(8,128)(2,1)} %bitcast.7, bf16[1024,128]{1,0:T(8,128)(2,1)} %table_hbm.1), custom_call_target="tpu_custom_call" | custom-call | tf_op jit(solution)/shard_map/outer_product_mean/pallas_call | solution.py:348
  24.0 1.7 %copy.8 = bf16[64,16,128]{2,1,0:T(8,128)(2,1)} copy(bf16[64,16,128]{2,1,0:T(8,128)(2,1)} %outer_product_mean.1) | data formatting | bytes 524288

commit v4 on v3

--- a/solution.py
+++ b/solution.py
@@ -73,8 +73,8 @@
 
 F32 = jnp.float32
 BF16 = jnp.bfloat16
-CHUNKS = 2
-VMEM_BYTES = 63 * 1024 * 1024
+CHUNKS = 4
+VMEM_BYTES = 40 * 1024 * 1024
 MESH = pl.DeviceIdType.MESH
 
 
@@ -169,11 +169,11 @@
     def each_hop(q, hop, act_below, act_above):
         @pl.when(z >= hop)
         def _():
-            act_below(blk - 2 * hop, q, hop)
+            act_below(blk - 2 * hop, q)
 
         @pl.when(z + hop < nz)
         def _():
-            act_above(blk + 2 * hop, q, hop)
+            act_above(blk + 2 * hop, q)
 
     for q in range(CHUNKS):
         cross(blk, q).start()
@@ -205,42 +205,19 @@
         norm = jrow * rmask_ref[blk * res + i].astype(F32) * count
         inv[i:i + 1, :] = 1.0 / jnp.maximum(norm, 1.0)
 
-    even = z % 2 == 0
     last = CHUNKS - 1
-    mate = blk + 2 - 4 * (z % 2)
-
-    def relay(block):
-        return copy(block, last, 3, mate)
-
-    def cross_below(block, q, hop, act):
-        if hop == 1 and q == last:
-            pl.when(even)(lambda: act(cross(block, q)))
-        else:
-            act(cross(block, q))
-
-    def cross_above(block, q, hop, act):
-        if hop == 1 and q == last:
-            pl.when(z % 2 == 1)(lambda: act(cross(block, q)))
-        else:
-            act(cross(block, q))
-
-    def start(made):
-        made.start()
-
-    def sent(made):
-        made.wait_send()
-
-    def from_below(block, q, hop):
+
+    def from_below(block, q):
         copy(block, q, 0, blk).wait_recv()
-        cross_below(block, q, hop, start)
+        cross(block, q).start()
 
         @pl.when(z < nz - 1)
         def _():
             up(block, q).start()
 
-    def from_above(block, q, hop):
+    def from_above(block, q):
         copy(block, q, 1, blk).wait_recv()
-        cross_above(block, q, hop, start)
+        cross(block, q).start()
 
         @pl.when(z > 0)
         def _():
@@ -249,9 +226,6 @@
     for hop in range(1, nz):
         for q in range(CHUNKS):
             each_hop(q, hop, from_below, from_above)
-        if hop == 1:
-            copy(across, last, 2, blk).wait_recv()
-            relay(across).start()
 
     def swap(h):
         return pltpu.make_async_remote_copy(
@@ -264,12 +238,7 @@
     pairs = res // 2
     for q in range(CHUNKS):
         for k in range(nz):
-            if q == last:
-                @pl.when(z != k)
-                def _():
-                    copy(2 * k + 1 - side, q, 2, blk).wait_recv()
-            else:
-                copy(2 * k + 1 - side, q, 2, blk).wait_recv()
+            copy(2 * k + 1 - side, q, 2, blk).wait_recv()
         base = q * part
         for k in range(base, base + part, 2):
             right_k = jnp.concatenate(
@@ -280,10 +249,14 @@
             for u in range(2):
                 piece = outer[:, u * cols:(u + 1) * cols].reshape(res, width, cols)
                 outer_ref[:, (k + u) * width:(k + u + 1) * width, :] = piece
-        table_q = table_t[:, base * width:(base + part) * width]
+        if q < last - 1:
+            continue
+        first = 0 if q < last else base * width
+        depth = (base + part) * width
+        table_q = table_t[:, first:depth]
         for p in range(pairs):
             both = [
-                outer_ref[p * 2 + u, base * width:(base + part) * width, :] for u in range(2)
+                outer_ref[p * 2 + u, first:depth, :] for u in range(2)
             ]
             term = jnp.dot(table_q, jnp.concatenate(both, axis=1), preferred_element_type=F32)
             for u in range(2):
@@ -291,21 +264,21 @@
                 at = pl.ds(i % 8, pair // 2, stride=8)
                 for g in range(2):
                     piece = term[g * (pair // 2):(g + 1) * (pair // 2), u * cols:(u + 1) * cols]
-                    if q > 0:
+                    if q == last:
                         piece = piece + acc[g, i // 8, at, :]
                     acc[g, i // 8, at, :] = piece
             if q == last and p % 4 == 3:
                 swap(p // 4).start()
 
-    def sent_below(block, q, hop):
-        cross_below(block, q, hop, sent)
+    def sent_below(block, q):
+        cross(block, q).wait_send()
 
         @pl.when(z < nz - 1)
         def _():
             up(block, q).wait_send()
 
-    def sent_above(block, q, hop):
-        cross_above(block, q, hop, sent)
+    def sent_above(block, q):
+        cross(block, q).wait_send()
 
         @pl.when(z > 0)
         def _():
@@ -324,7 +297,6 @@
 
         for hop in range(1, nz):
             each_hop(q, hop, sent_below, sent_above)
-    relay(across).wait_send()
 
     sums = []
     for h in range(res // 8):
@@ -369,7 +341,7 @@
             pltpu.VMEM((res, cols), F32),
             pltpu.SemaphoreType.DMA((10,)),
             pltpu.SemaphoreType.DMA((nblk, CHUNKS)),
-            pltpu.SemaphoreType.DMA((4, nblk, CHUNKS)),
+            pltpu.SemaphoreType.DMA((3, nblk, CHUNKS)),
             pltpu.SemaphoreType.DMA((2, res // 8)),
         ],
         compiler_params=pltpu.CompilerParams(
@@ -377,13 +349,18 @@
         ),
         name="outer_product_mean",
     )(
-        alignment_activity.transpose(1, 2, 0),
-        sequence_mask.reshape(1, rows),
-        residue_mask.reshape(1, cols),
-        residue_mask,
-        lower_weights.T,
-        upper_weights.T,
-        output_projector,
+        *[
+            pltpu.with_memory_space_constraint(array, pltpu.HBM)
+            for array in (
+                alignment_activity.transpose(1, 2, 0),
+                sequence_mask.reshape(1, rows),
+                residue_mask.reshape(1, cols),
+                residue_mask,
+                lower_weights.T,
+                upper_weights.T,
+                output_projector,
+            )
+        ]
     )
 
 

time: 25.8 us -> 23.3 us (0.903)
  Pallas kernels: 24 us -> 22.4 us
  local copies, waits for them, and re-layouts: 1.67 us -> 0.71 us
    pallas_call x1, Pallas kernels: 24 us -> 22.4 us  [fused_shards(): pl.pallas_call(functools.partial(fused, (nblk, rows, res, feat, width)),...]
    unnamed x1, local copies, waits for them, and re-layouts: 1.67 us -> 0.71 us
where the time goes in v4:
time: 23.3 us; the launch traced here: 23.1 us
  Pallas kernels  22.4 us (96%)
  local copies, waits for them, and re-layouts  0.71 us (3%)
    pallas_call x1, Pallas kernels, fused_shards(): pl.pallas_call(functools.partial(fused, (nblk, rows, res, feat, width)),...  22.4 us
    unnamed x1, local copies, waits for them, and re-layouts  0.71 us

profile of v4, /device:TPU:0, one launch (start us, length us, event | category | flops | bytes accessed | tf_op | source)
XLA Modules:
  0.0 23.1 jit_solution(11921469919262745132)
XLA Ops:
  0.0 22.4 %outer_product_mean.1 = bf16[64,16,128]{2,1,0:T(8,128)(2,1)S(1)} custom-call(bf16[16,64,256]{2,1,0:T(8,128)(2,1)} %bitcast.5, s32[1,256]{1,0:T(1,128)} %bitcast.9, s32[1,128]{1,0:T(1,128)} %bitcast.8, s32[128]{0:T(128)} %rmask_hbm.1, bf16[32,64]{1,0:T(8,128)(2,1)} %bitcast.6, bf16[32,64]{1,0:T(8,128)(2,1)} %bitcast.7, bf16[1024,128]{1,0:T(8,128)(2,1)} %table_hbm.1), custom_call_target="tpu_custom_call" | custom-call | tf_op jit(solution)/shard_map/outer_product_mean/pallas_call | solution.py:320
  22.4 0.7 %copy.8 = bf16[64,16,128]{2,1,0:T(8,128)(2,1)} copy(bf16[64,16,128]{2,1,0:T(8,128)(2,1)S(1)} %outer_product_mean.1) | data formatting | bytes 524288
